TPU v7x, 256 devices: a whole 4x4x8 slice. The times are simulated.
256 devices in a mesh: row: 32 (over y, z), col: 8 (over x, core).
Axes of the slice: x: 4, y: 4, z: 8, core: 2. Of those that a mesh axis runs over, the one named last changes fastest.
Arguments:
- lower: float32 [6, 2048, 2048], P(None, 'row', 'col'), may hold values from -0.046875 to 0.046875
- dinv: float32 [4, 2048, 2048], P(None, 'row', 'col'), as said below
- kcols: float32 [4, 2048, 2048], P(None, 'row', 'col'), may hold values from -6 to 6
- prior: float32 [2048], P('col'), may hold values from 3 to 5
Outputs:
- solved_columns: float32 [4, 2048, 2048], P(None, 'row', 'col')
- variance: float32 [2048], P('col')
Inputs may be any that keep to these rules, and one draw needn't show every extreme that they name: Each block of dinv is lower triangular with a positive diagonal.
All inputs are finite; a program needn't handle non-finite values.
Results may differ from a plain program's by a relative error of at most 0.0001.
Values sent between devices are 32-bit elements; how exact they have to be, the bound alone decides.
A program may use at most 64 MiB of HBM per device.

v0:
```python
import jax
import jax.numpy as jnp
from jax import lax
from jax.sharding import PartitionSpec as P

OBS = 8192


def append_block(gathered, section):
    return jnp.dot(
        section, gathered, precision=lax.Precision.HIGHEST, preferred_element_type=jnp.float32
    )


def remove_block(gathered, running, section):
    return running - jnp.dot(
        section, gathered, precision=lax.Precision.HIGHEST, preferred_element_type=jnp.float32
    )


def body(lower, dinv, kcols, prior):
    segments = kcols.shape[0]
    breadth = kcols.shape[2]
    bounds = [(0, breadth)]
    pending = [
        [kcols[segment_now, :, bound_pair[0] : bound_pair[1]] for segment_now in range(segments)]
        for bound_pair in bounds
    ]
    spread = [[] for bound_pair in bounds]
    solved = [[] for bound_pair in bounds]
    for segment_now in range(segments):
        residual = pending[0][segment_now]
        for earlier in range(segment_now):
            residual = remove_block(
                spread[0][earlier],
                residual,
                lax.all_gather(
                    lower[segment_now * (segment_now - 1) // 2 + earlier], "col", axis=1, tiled=True
                ),
            )
        whole_residual = lax.all_gather(residual, "row", axis=0, tiled=True)
        answer = append_block(
            whole_residual, lax.all_gather(dinv[segment_now], "col", axis=1, tiled=True)
        )
        solved[0].append(answer)
        if segment_now + 1 < segments:
            whole_answer = lax.all_gather(answer, "row", axis=0, tiled=True)
            spread[0].append(whole_answer)
    columns = [solved[0][segment_now] for segment_now in range(segments)]
    solution = jnp.stack(columns)
    squares = jnp.sum(solution * solution, axis=(0, 1))
    totals = lax.psum(squares, "row")
    variance = prior - totals / OBS
    return (solution, variance)


def solution(mesh):
    in_specs = (P(None, "row", "col"), P(None, "row", "col"), P(None, "row", "col"), P("col"))
    out_specs = (P(None, "row", "col"), P("col"))
    return jax.shard_map(body, mesh=mesh, in_specs=in_specs, out_specs=out_specs, check_vma=False)
```

profile of v0, /device:TPU:2, one launch (start us, length us, event | category | flops | bytes accessed | tf_op | source)
XLA Modules:
  0.0 652.7 jit_solution(342715879217123548)
XLA Ops:
  7.2 0.0 copy-start.4
  7.2 0.0 all-gather.31.cloned.1.call-start
  7.2 1.5 slice.43
  8.7 0.0 all-gather.31.cloned.1.call-update
  8.8 0.0 all-gather.19.cloned.1.call-start
  8.8 1.0 fusion.21
  9.8 13.2 %all-gather = f32[1,64,2048]{2,1,0:T(8,128)S(1)} all-gather(f32[1,64,256]{2,1,0:T(8,128)S(1)} %get-tuple-element.12), channel_id=2, replica_groups=mesh['row'=32,'col'=8] {'col'}, dimensions={2}, use_global_device_ids=true | all-gather | bytes 589824 | tf_op jit(solution)/shard_map/all_gather | solution.py:43
  22.9 69.1 %all-gather.31.cloned.1.call-done = f32[1,2048,256]{2,1,0:T(8,128)} async-done(((f32[1,64,256]{2,1,0:T(8,128)}), f32[1,2048,256]{2,1,0:T(8,128)}) %all-gather.31.cloned.1.call-update) | async-done | bytes 2097168 | tf_op jit(solution)/shard_map/all_gather | solution.py:41
  92.1 3.4 fusion
  95.5 0.0 all-gather.19.cloned.1.call-update
  95.5 0.0 all-gather.21.cloned.1.call-start
  95.5 0.0 copy-done.4
  95.6 13.1 %all-gather.2 = f32[1,64,2048]{2,1,0:T(8,128)S(1)} all-gather(f32[1,64,256]{2,1,0:T(8,128)S(1)} %get-tuple-element.7), channel_id=4, replica_groups=mesh['row'=32,'col'=8] {'col'}, dimensions={2}, use_global_device_ids=true | all-gather | bytes 589824 | tf_op jit(solution)/shard_map/all_gather | solution.py:37
  108.7 62.1 %all-gather.19.cloned.1.call-done = f32[2048,256]{1,0:T(8,128)} async-done(((f32[64,256]{1,0:T(8,128)}), f32[2048,256]{1,0:T(8,128)}) %all-gather.19.cloned.1.call-update) | async-done | bytes 2097168 | tf_op jit(solution)/shard_map/all_gather | solution.py:47
  170.8 3.6 fusion.2
  174.3 0.0 all-gather.21.cloned.1.call-update
  174.4 0.0 all-gather.23.cloned.1.call-start
  174.4 13.1 %all-gather.3 = f32[1,64,2048]{2,1,0:T(8,128)S(1)} all-gather(f32[1,64,256]{2,1,0:T(8,128)S(1)} %get-tuple-element.11), channel_id=5, replica_groups=mesh['row'=32,'col'=8] {'col'}, dimensions={2}, use_global_device_ids=true | all-gather | bytes 589824 | tf_op jit(solution)/shard_map/all_gather | solution.py:43
  187.5 62.1 %all-gather.21.cloned.1.call-done = f32[2048,256]{1,0:T(8,128)} async-done(((f32[64,256]{1,0:T(8,128)}), f32[2048,256]{1,0:T(8,128)}) %all-gather.21.cloned.1.call-update) | async-done | bytes 2097168 | tf_op jit(solution)/shard_map/all_gather | solution.py:41
  249.7 3.6 fusion.16
  253.2 0.0 copy-start
  253.2 0.0 all-gather.23.cloned.1.call-update
  253.2 0.0 all-gather.25.cloned.1.call-start
  253.3 13.3 %all-gather.5 = f32[1,64,2048]{2,1,0:T(8,128)S(1)} all-gather(f32[1,64,256]{2,1,0:T(8,128)S(1)} %get-tuple-element.5), channel_id=7, replica_groups=mesh['row'=32,'col'=8] {'col'}, dimensions={2}, use_global_device_ids=true | all-gather | bytes 589824 | tf_op jit(solution)/shard_map/all_gather | solution.py:37
  266.5 13.1 %all-gather.4 = f32[1,64,2048]{2,1,0:T(8,128)S(1)} all-gather(f32[1,64,256]{2,1,0:T(8,128)S(1)} %get-tuple-element.6), channel_id=6, replica_groups=mesh['row'=32,'col'=8] {'col'}, dimensions={2}, use_global_device_ids=true | all-gather | bytes 589824 | tf_op jit(solution)/shard_map/all_gather | solution.py:37
  279.6 48.9 %all-gather.23.cloned.1.call-done = f32[2048,256]{1,0:T(8,128)} async-done(((f32[64,256]{1,0:T(8,128)}), f32[2048,256]{1,0:T(8,128)}) %all-gather.23.cloned.1.call-update) | async-done | bytes 2097168 | tf_op jit(solution)/shard_map/all_gather | solution.py:47
  328.5 2.9 convolution_bitcast_fusion.4
  331.4 0.0 copy-done
  331.4 2.8 fusion.4
  334.3 0.0 all-gather.25.cloned.1.call-update
  334.3 0.0 all-gather.27.cloned.1.call-start
  334.3 13.1 %all-gather.6 = f32[1,64,2048]{2,1,0:T(8,128)S(1)} all-gather(f32[1,64,256]{2,1,0:T(8,128)S(1)} %get-tuple-element.13), channel_id=8, replica_groups=mesh['row'=32,'col'=8] {'col'}, dimensions={2}, use_global_device_ids=true | all-gather | bytes 589824 | tf_op jit(solution)/shard_map/all_gather | solution.py:43
  347.4 62.1 %all-gather.25.cloned.1.call-done = f32[2048,256]{1,0:T(8,128)} async-done(((f32[64,256]{1,0:T(8,128)}), f32[2048,256]{1,0:T(8,128)}) %all-gather.25.cloned.1.call-update) | async-done | bytes 2097168 | tf_op jit(solution)/shard_map/all_gather | solution.py:41
  409.6 3.6 fusion.12
  413.1 0.0 all-gather.27.cloned.1.call-update
  413.2 0.0 all-gather.29.cloned.1.call-start
  413.2 13.1 %all-gather.9 = f32[1,64,2048]{2,1,0:T(8,128)S(1)} all-gather(f32[1,64,256]{2,1,0:T(8,128)S(1)} %get-tuple-element.8), channel_id=11, replica_groups=mesh['row'=32,'col'=8] {'col'}, dimensions={2}, use_global_device_ids=true | all-gather | bytes 589824 | tf_op jit(solution)/shard_map/all_gather | solution.py:37
  426.3 13.3 %all-gather.8 = f32[1,64,2048]{2,1,0:T(8,128)S(1)} all-gather(f32[1,64,256]{2,1,0:T(8,128)S(1)} %get-tuple-element.9), channel_id=10, replica_groups=mesh['row'=32,'col'=8] {'col'}, dimensions={2}, use_global_device_ids=true | all-gather | bytes 589824 | tf_op jit(solution)/shard_map/all_gather | solution.py:37
  439.6 13.1 %all-gather.7 = f32[1,64,2048]{2,1,0:T(8,128)S(1)} all-gather(f32[1,64,256]{2,1,0:T(8,128)S(1)} %get-tuple-element.4), channel_id=9, replica_groups=mesh['row'=32,'col'=8] {'col'}, dimensions={2}, use_global_device_ids=true | all-gather | bytes 589824 | tf_op jit(solution)/shard_map/all_gather | solution.py:37
  452.7 2.9 convolution_bitcast_fusion.2
  455.6 32.8 %all-gather.27.cloned.1.call-done = f32[2048,256]{1,0:T(8,128)} async-done(((f32[64,256]{1,0:T(8,128)}), f32[2048,256]{1,0:T(8,128)}) %all-gather.27.cloned.1.call-update) | async-done | bytes 2097168 | tf_op jit(solution)/shard_map/all_gather | solution.py:47
  488.4 2.9 convolution_bitcast_fusion.1
  491.3 2.8 fusion.7
  494.2 0.0 copy-start.1
  494.2 0.0 copy-start.2
  494.2 0.0 copy-start.3
  494.2 0.0 copy-start.5
  494.2 0.0 all-gather.29.cloned.1.call-update
  494.2 13.3 %all-gather.10 = f32[1,64,2048]{2,1,0:T(8,128)S(1)} all-gather(f32[1,64,256]{2,1,0:T(8,128)S(1)} %get-tuple-element.10), channel_id=12, replica_groups=mesh['row'=32,'col'=8] {'col'}, dimensions={2}, use_global_device_ids=true | all-gather | bytes 589824 | tf_op jit(solution)/shard_map/all_gather | solution.py:43
  507.4 62.0 %all-gather.29.cloned.1.call-done = f32[2048,256]{1,0:T(8,128)} async-done(((f32[64,256]{1,0:T(8,128)}), f32[2048,256]{1,0:T(8,128)}) %all-gather.29.cloned.1.call-update) | async-done | bytes 2097168 | tf_op jit(solution)/shard_map/all_gather | solution.py:41
  569.5 2.9 convolution_bitcast_fusion
  572.4 0.0 copy-done.1
  572.4 0.0 copy-done.2
  572.4 0.0 copy-done.3
  572.4 0.7 multiply_reduce_fusion
  573.2 72.1 %psum.7 = f32[256]{0:T(256)S(1)} all-reduce(f32[256]{0:T(256)S(1)} %get-tuple-element.2), channel_id=1, replica_groups=mesh['row'=32,'col'=8] {'row'}, use_global_device_ids=true, to_apply=%region_1.0 | all-reduce | flops 256 | bytes 2048 | tf_op jit(solution)/shard_map/psum | solution.py:52
  645.3 0.0 copy-done.5
  645.3 0.6 multiply_subtract_fusion
  (1 shorter events, 0.0 us)
Async XLA Ops:
  7.2 88.4 %copy-start.4 = (f32[6,64,256]{2,1,0:T(8,128)S(1)}, f32[6,64,256]{2,1,0:T(8,128)}, u32[]{:S(2)}) copy-start(f32[6,64,256]{2,1,0:T(8,128)} %param.4) | copy-start | bytes 1179652
  7.2 84.9 %all-gather.31.cloned.1.call-start = ((), (), s32[]{:S(2)}) async-start(), calls=%async_computation.6 | async-start | bytes 2162688 | tf_op jit(solution)/shard_map/all_gather | solution.py:41
  8.8 162.0 %all-gather.19.cloned.1.call-start = ((), (), s32[]{:S(2)}) async-start(), calls=%async_computation | async-start | bytes 2162688 | tf_op jit(solution)/shard_map/all_gather | solution.py:47
  95.5 154.2 %all-gather.21.cloned.1.call-start = ((), (), s32[]{:S(2)}) async-start(), calls=%async_computation.1 | async-start | bytes 2162688 | tf_op jit(solution)/shard_map/all_gather | solution.py:41
  174.4 154.1 %all-gather.23.cloned.1.call-start = ((), (), s32[]{:S(2)}) async-start(), calls=%async_computation.2 | async-start | bytes 2162688 | tf_op jit(solution)/shard_map/all_gather | solution.py:47
  253.2 78.2 %copy-start = (f32[2048,256]{1,0:T(8,128)S(1)}, f32[2048,256]{1,0:T(8,128)}, u32[]{:S(2)}) copy-start(f32[2048,256]{1,0:T(8,128)} %all-gather.19.cloned.1.call-done) | copy-start | bytes 6291460
  253.2 156.3 %all-gather.25.cloned.1.call-start = ((), (), s32[]{:S(2)}) async-start(), calls=%async_computation.3 | async-start | bytes 2162688 | tf_op jit(solution)/shard_map/all_gather | solution.py:41
  334.3 154.1 %all-gather.27.cloned.1.call-start = ((), (), s32[]{:S(2)}) async-start(), calls=%async_computation.4 | async-start | bytes 2162688 | tf_op jit(solution)/shard_map/all_gather | solution.py:47
  413.2 156.3 %all-gather.29.cloned.1.call-start = ((), (), s32[]{:S(2)}) async-start(), calls=%async_computation.5 | async-start | bytes 2162688 | tf_op jit(solution)/shard_map/all_gather | solution.py:41
  494.2 78.3 %copy-start.1 = (f32[64,256]{1,0:T(8,128)S(1)}, f32[64,256]{1,0:T(8,128)}, u32[]{:S(2)}) copy-start(f32[64,256]{1,0:T(8,128)} %fusion) | copy-start | bytes 196612
  494.2 78.3 %copy-start.2 = (f32[256,64]{0,1:T(8,128)S(1)}, f32[256,64]{0,1:T(8,128)}, u32[]{:S(2)}) copy-start(f32[256,64]{0,1:T(8,128)} %fusion.16) | copy-start | bytes 196612
  494.2 78.3 %copy-start.3 = (f32[256,64]{0,1:T(8,128)S(1)}, f32[256,64]{0,1:T(8,128)}, u32[]{:S(2)}) copy-start(f32[256,64]{0,1:T(8,128)} %fusion.12) | copy-start | bytes 196612
  494.2 151.1 %copy-start.5 = (f32[256]{0:T(256)S(1)}, f32[256]{0:T(256)}, u32[]{:S(2)}) copy-start(f32[256]{0:T(256)} %param.7) | copy-start | bytes 3076
Sparse Core Ops, SparseCore 0:
  11.2 80.8 all-gather.30
  95.6 75.1 all-gather.18
  174.5 75.1 all-gather.20
  253.4 75.0 all-gather.22
  334.4 75.1 all-gather.24
  413.3 75.0 all-gather.26
  494.3 75.1 all-gather.28
where the time goes:
time: 653 us
  waiting for transfers between devices  399 us (61%)
  blocking collectives  204 us (31%)
  matrix products  31.4 us (5%)
  between operations  14.2 us (2%)
    all_gather x4, waiting for transfers between devices, body(): whole_residual = lax.all_gather(residual, 'row', axis=0, tiled=True)  255 us
    all_gather x3, waiting for transfers between devices, body(): whole_answer = lax.all_gather(answer, 'row', axis=0, tiled=True)  144 us
    all_gather x6, blocking collectives, body(): lax.all_gather(lower[segment_now * (segment_now - 1) // 2 + earlier], 'co...  78.9 us
    psum x1, blocking collectives, body(): totals = lax.psum(squares, 'row')  72.1 us
    all_gather x4, blocking collectives, body(): lax.all_gather(dinv[segment_now], 'col', axis=1, tiled=True)  52.7 us
    dot_general x6, matrix products, remove_block(): jnp.dot(section, gathered, precision=lax.Precision.HIGHEST, preferred_ele...  18 us
    dot_general x4, matrix products, append_block(): jnp.dot(section, gathered, precision=lax.Precision.HIGHEST, preferred_ele...  13.4 us
  transfers between devices with their start and end apart: 7, of which 7 were waited for; matrix products, arithmetic and copies ran while one was open for 1% of the time, Pallas kernels for 0%

commit v1 on v0

--- a/solution.py
+++ b/solution.py
@@ -49,7 +49,8 @@
     columns = [solved[0][segment_now] for segment_now in range(segments)]
     solution = jnp.stack(columns)
     squares = jnp.sum(solution * solution, axis=(0, 1))
-    totals = lax.psum(squares, "row")
+    pieces = lax.all_gather(squares, "row", axis=0, tiled=False)
+    totals = pieces.sum(axis=0)
     variance = prior - totals / OBS
     return (solution, variance)
 

time: 653 us -> 623 us (0.954)
  blocking collectives: 204 us -> 173 us
    psum x1 -> x0, blocking collectives: 72.1 us -> none  [body(): totals = lax.psum(squares, 'row')]
    all_gather x0 -> x1, blocking collectives: none -> 41.4 us  [body(): pieces = lax.all_gather(squares, 'row', axis=0, tiled=False)]
where the time goes in v1:
time: 623 us; the launch traced here: 622 us
  waiting for transfers between devices  399 us (64%)
  blocking collectives  173 us (28%)
  matrix products  31.4 us (5%)
  between operations  14.2 us (2%)
    all_gather x4, waiting for transfers between devices, body(): whole_residual = lax.all_gather(residual, 'row', axis=0, tiled=True)  255 us
    all_gather x3, waiting for transfers between devices, body(): whole_answer = lax.all_gather(answer, 'row', axis=0, tiled=True)  144 us
    all_gather x6, blocking collectives, body(): lax.all_gather(lower[segment_now * (segment_now - 1) // 2 + earlier], 'co...  78.9 us
    all_gather x4, blocking collectives, body(): lax.all_gather(dinv[segment_now], 'col', axis=1, tiled=True)  52.7 us
    all_gather x1, blocking collectives, body(): pieces = lax.all_gather(squares, 'row', axis=0, tiled=False)  41.4 us
    dot_general x6, matrix products, remove_block(): jnp.dot(section, gathered, precision=lax.Precision.HIGHEST, preferred_ele...  18 us
    dot_general x4, matrix products, append_block(): jnp.dot(section, gathered, precision=lax.Precision.HIGHEST, preferred_ele...  13.4 us
  transfers between devices with their start and end apart: 7, of which 7 were waited for; matrix products, arithmetic and copies ran while one was open for 1% of the time, Pallas kernels for 0%

profile of v1, /device:TPU:2, one launch (start us, length us, event | category | flops | bytes accessed | tf_op | source)
XLA Modules:
  0.0 622.0 jit_solution(9787383809575806575)
XLA Ops:
  7.2 0.0 copy-start.4
  7.2 0.0 all-gather.33.cloned.1.call-start
  7.2 1.5 slice.43
  8.7 0.0 all-gather.33.cloned.1.call-update
  8.8 0.0 all-gather.21.cloned.1.call-start
  8.8 1.0 fusion.21
  9.8 13.2 %all-gather = f32[1,64,2048]{2,1,0:T(8,128)S(1)} all-gather(f32[1,64,256]{2,1,0:T(8,128)S(1)} %get-tuple-element.12), channel_id=2, replica_groups=mesh['row'=32,'col'=8] {'col'}, dimensions={2}, use_global_device_ids=true | all-gather | bytes 589824 | tf_op jit(solution)/shard_map/all_gather | solution.py:43
  22.9 69.1 %all-gather.33.cloned.1.call-done = f32[1,2048,256]{2,1,0:T(8,128)} async-done(((f32[1,64,256]{2,1,0:T(8,128)}), f32[1,2048,256]{2,1,0:T(8,128)}) %all-gather.33.cloned.1.call-update) | async-done | bytes 2097168 | tf_op jit(solution)/shard_map/all_gather | solution.py:41
  92.1 3.4 fusion
  95.5 0.0 all-gather.21.cloned.1.call-update
  95.5 0.0 all-gather.23.cloned.1.call-start
  95.5 0.0 copy-done.4
  95.6 13.1 %all-gather.2 = f32[1,64,2048]{2,1,0:T(8,128)S(1)} all-gather(f32[1,64,256]{2,1,0:T(8,128)S(1)} %get-tuple-element.7), channel_id=4, replica_groups=mesh['row'=32,'col'=8] {'col'}, dimensions={2}, use_global_device_ids=true | all-gather | bytes 589824 | tf_op jit(solution)/shard_map/all_gather | solution.py:37
  108.7 62.1 %all-gather.21.cloned.1.call-done = f32[2048,256]{1,0:T(8,128)} async-done(((f32[64,256]{1,0:T(8,128)}), f32[2048,256]{1,0:T(8,128)}) %all-gather.21.cloned.1.call-update) | async-done | bytes 2097168 | tf_op jit(solution)/shard_map/all_gather | solution.py:47
  170.8 3.6 fusion.2
  174.3 0.0 all-gather.23.cloned.1.call-update
  174.4 0.0 all-gather.25.cloned.1.call-start
  174.4 13.1 %all-gather.3 = f32[1,64,2048]{2,1,0:T(8,128)S(1)} all-gather(f32[1,64,256]{2,1,0:T(8,128)S(1)} %get-tuple-element.11), channel_id=5, replica_groups=mesh['row'=32,'col'=8] {'col'}, dimensions={2}, use_global_device_ids=true | all-gather | bytes 589824 | tf_op jit(solution)/shard_map/all_gather | solution.py:43
  187.5 62.1 %all-gather.23.cloned.1.call-done = f32[2048,256]{1,0:T(8,128)} async-done(((f32[64,256]{1,0:T(8,128)}), f32[2048,256]{1,0:T(8,128)}) %all-gather.23.cloned.1.call-update) | async-done | bytes 2097168 | tf_op jit(solution)/shard_map/all_gather | solution.py:41
  249.7 3.6 fusion.16
  253.2 0.0 copy-start
  253.2 0.0 all-gather.25.cloned.1.call-update
  253.2 0.0 all-gather.27.cloned.1.call-start
  253.3 13.3 %all-gather.5 = f32[1,64,2048]{2,1,0:T(8,128)S(1)} all-gather(f32[1,64,256]{2,1,0:T(8,128)S(1)} %get-tuple-element.5), channel_id=7, replica_groups=mesh['row'=32,'col'=8] {'col'}, dimensions={2}, use_global_device_ids=true | all-gather | bytes 589824 | tf_op jit(solution)/shard_map/all_gather | solution.py:37
  266.5 13.1 %all-gather.4 = f32[1,64,2048]{2,1,0:T(8,128)S(1)} all-gather(f32[1,64,256]{2,1,0:T(8,128)S(1)} %get-tuple-element.6), channel_id=6, replica_groups=mesh['row'=32,'col'=8] {'col'}, dimensions={2}, use_global_device_ids=true | all-gather | bytes 589824 | tf_op jit(solution)/shard_map/all_gather | solution.py:37
  279.6 48.9 %all-gather.25.cloned.1.call-done = f32[2048,256]{1,0:T(8,128)} async-done(((f32[64,256]{1,0:T(8,128)}), f32[2048,256]{1,0:T(8,128)}) %all-gather.25.cloned.1.call-update) | async-done | bytes 2097168 | tf_op jit(solution)/shard_map/all_gather | solution.py:47
  328.5 2.9 convolution_bitcast_fusion.4
  331.4 0.0 copy-done
  331.4 2.8 fusion.4
  334.3 0.0 all-gather.27.cloned.1.call-update
  334.3 0.0 all-gather.29.cloned.1.call-start
  334.3 13.1 %all-gather.6 = f32[1,64,2048]{2,1,0:T(8,128)S(1)} all-gather(f32[1,64,256]{2,1,0:T(8,128)S(1)} %get-tuple-element.13), channel_id=8, replica_groups=mesh['row'=32,'col'=8] {'col'}, dimensions={2}, use_global_device_ids=true | all-gather | bytes 589824 | tf_op jit(solution)/shard_map/all_gather | solution.py:43
  347.4 62.1 %all-gather.27.cloned.1.call-done = f32[2048,256]{1,0:T(8,128)} async-done(((f32[64,256]{1,0:T(8,128)}), f32[2048,256]{1,0:T(8,128)}) %all-gather.27.cloned.1.call-update) | async-done | bytes 2097168 | tf_op jit(solution)/shard_map/all_gather | solution.py:41
  409.6 3.6 fusion.12
  413.1 0.0 all-gather.29.cloned.1.call-update
  413.2 0.0 all-gather.31.cloned.1.call-start
  413.2 13.1 %all-gather.9 = f32[1,64,2048]{2,1,0:T(8,128)S(1)} all-gather(f32[1,64,256]{2,1,0:T(8,128)S(1)} %get-tuple-element.8), channel_id=11, replica_groups=mesh['row'=32,'col'=8] {'col'}, dimensions={2}, use_global_device_ids=true | all-gather | bytes 589824 | tf_op jit(solution)/shard_map/all_gather | solution.py:37
  426.3 13.3 %all-gather.8 = f32[1,64,2048]{2,1,0:T(8,128)S(1)} all-gather(f32[1,64,256]{2,1,0:T(8,128)S(1)} %get-tuple-element.9), channel_id=10, replica_groups=mesh['row'=32,'col'=8] {'col'}, dimensions={2}, use_global_device_ids=true | all-gather | bytes 589824 | tf_op jit(solution)/shard_map/all_gather | solution.py:37
  439.6 13.1 %all-gather.7 = f32[1,64,2048]{2,1,0:T(8,128)S(1)} all-gather(f32[1,64,256]{2,1,0:T(8,128)S(1)} %get-tuple-element.4), channel_id=9, replica_groups=mesh['row'=32,'col'=8] {'col'}, dimensions={2}, use_global_device_ids=true | all-gather | bytes 589824 | tf_op jit(solution)/shard_map/all_gather | solution.py:37
  452.7 2.9 convolution_bitcast_fusion.2
  455.6 32.8 %all-gather.29.cloned.1.call-done = f32[2048,256]{1,0:T(8,128)} async-done(((f32[64,256]{1,0:T(8,128)}), f32[2048,256]{1,0:T(8,128)}) %all-gather.29.cloned.1.call-update) | async-done | bytes 2097168 | tf_op jit(solution)/shard_map/all_gather | solution.py:47
  488.4 2.9 convolution_bitcast_fusion.1
  491.3 2.8 fusion.7
  494.2 0.0 copy-start.1
  494.2 0.0 copy-start.2
  494.2 0.0 copy-start.3
  494.2 0.0 copy-start.5
  494.2 0.0 all-gather.31.cloned.1.call-update
  494.2 13.3 %all-gather.10 = f32[1,64,2048]{2,1,0:T(8,128)S(1)} all-gather(f32[1,64,256]{2,1,0:T(8,128)S(1)} %get-tuple-element.10), channel_id=12, replica_groups=mesh['row'=32,'col'=8] {'col'}, dimensions={2}, use_global_device_ids=true | all-gather | bytes 589824 | tf_op jit(solution)/shard_map/all_gather | solution.py:43
  507.4 62.0 %all-gather.31.cloned.1.call-done = f32[2048,256]{1,0:T(8,128)} async-done(((f32[64,256]{1,0:T(8,128)}), f32[2048,256]{1,0:T(8,128)}) %all-gather.31.cloned.1.call-update) | async-done | bytes 2097168 | tf_op jit(solution)/shard_map/all_gather | solution.py:41
  569.5 2.9 convolution_bitcast_fusion
  572.4 0.0 copy-done.1
  572.4 0.0 copy-done.2
  572.4 0.0 copy-done.3
  572.4 0.7 multiply_reduce_fusion
  573.2 41.4 %all-gather.12 = f32[32,1,256]{2,1,0:T(1,128)S(1)} all-gather(f32[1,1,256]{2,1,0:T(1,128)S(1)} %bitcast.89), channel_id=13, replica_groups=mesh['row'=32,'col'=8] {'row'}, dimensions={0}, use_global_device_ids=true | all-gather | bytes 33792 | tf_op jit(solution)/shard_map/all_gather | solution.py:52
  614.5 0.1 reduce_sum.19
  614.6 0.0 copy-done.5
  614.6 0.6 multiply_subtract_fusion
  (1 shorter events, 0.0 us)
Async XLA Ops:
  7.2 88.4 %copy-start.4 = (f32[6,64,256]{2,1,0:T(8,128)S(1)}, f32[6,64,256]{2,1,0:T(8,128)}, u32[]{:S(2)}) copy-start(f32[6,64,256]{2,1,0:T(8,128)} %param.4) | copy-start | bytes 1179652
  7.2 84.9 %all-gather.33.cloned.1.call-start = ((), (), s32[]{:S(2)}) async-start(), calls=%async_computation.6 | async-start | bytes 2162688 | tf_op jit(solution)/shard_map/all_gather | solution.py:41
  8.8 162.0 %all-gather.21.cloned.1.call-start = ((), (), s32[]{:S(2)}) async-start(), calls=%async_computation | async-start | bytes 2162688 | tf_op jit(solution)/shard_map/all_gather | solution.py:47
  95.5 154.2 %all-gather.23.cloned.1.call-start = ((), (), s32[]{:S(2)}) async-start(), calls=%async_computation.1 | async-start | bytes 2162688 | tf_op jit(solution)/shard_map/all_gather | solution.py:41
  174.4 154.1 %all-gather.25.cloned.1.call-start = ((), (), s32[]{:S(2)}) async-start(), calls=%async_computation.2 | async-start | bytes 2162688 | tf_op jit(solution)/shard_map/all_gather | solution.py:47
  253.2 78.2 %copy-start = (f32[2048,256]{1,0:T(8,128)S(1)}, f32[2048,256]{1,0:T(8,128)}, u32[]{:S(2)}) copy-start(f32[2048,256]{1,0:T(8,128)} %all-gather.21.cloned.1.call-done) | copy-start | bytes 6291460
  253.2 156.3 %all-gather.27.cloned.1.call-start = ((), (), s32[]{:S(2)}) async-start(), calls=%async_computation.3 | async-start | bytes 2162688 | tf_op jit(solution)/shard_map/all_gather | solution.py:41
  334.3 154.1 %all-gather.29.cloned.1.call-start = ((), (), s32[]{:S(2)}) async-start(), calls=%async_computation.4 | async-start | bytes 2162688 | tf_op jit(solution)/shard_map/all_gather | solution.py:47
  413.2 156.3 %all-gather.31.cloned.1.call-start = ((), (), s32[]{:S(2)}) async-start(), calls=%async_computation.5 | async-start | bytes 2162688 | tf_op jit(solution)/shard_map/all_gather | solution.py:41
  494.2 78.3 %copy-start.1 = (f32[64,256]{1,0:T(8,128)S(1)}, f32[64,256]{1,0:T(8,128)}, u32[]{:S(2)}) copy-start(f32[64,256]{1,0:T(8,128)} %fusion) | copy-start | bytes 196612
  494.2 78.3 %copy-start.2 = (f32[256,64]{0,1:T(8,128)S(1)}, f32[256,64]{0,1:T(8,128)}, u32[]{:S(2)}) copy-start(f32[256,64]{0,1:T(8,128)} %fusion.16) | copy-start | bytes 196612
  494.2 78.3 %copy-start.3 = (f32[256,64]{0,1:T(8,128)S(1)}, f32[256,64]{0,1:T(8,128)}, u32[]{:S(2)}) copy-start(f32[256,64]{0,1:T(8,128)} %fusion.12) | copy-start | bytes 196612
  494.2 120.4 %copy-start.5 = (f32[256]{0:T(256)S(1)}, f32[256]{0:T(256)}, u32[]{:S(2)}) copy-start(f32[256]{0:T(256)} %param.7) | copy-start | bytes 3076
Sparse Core Ops, SparseCore 0:
  11.2 80.8 all-gather.32
  95.6 75.1 all-gather.20
  174.5 75.1 all-gather.22
  253.4 75.0 all-gather.24
  334.4 75.1 all-gather.26
  413.3 75.0 all-gather.28
  494.3 75.1 all-gather.30
